TPU v7x, 256 devices: a whole 4x4x8 slice. The times are simulated.
256 devices in a mesh: cfg: 2 (over core), req: 16 (over x_hi, z), seq: 8 (over x_lo, y).
Axes of the slice: x: 4 (x_hi: 2, x_lo: 2; x = x_hi * 2 + x_lo), y: 4, z: 8, core: 2. Of those that a mesh axis runs over, the one named last changes fastest.
Arguments:
- hidden: bfloat16 [2, 16, 2304, 1536], P('cfg', 'req', 'seq'), may hold values from -6 to 6
- latent: float32 [16, 2304, 64], P('req', 'seq', 'cfg'), may hold values from -6 to 6
- modulation: float32 [16, 5, 1536], P('req'), may hold values from -3 to 3
- w_qkv: bfloat16 [1536, 4608], P('req'), may hold values from -1 to 1
- w_out: bfloat16 [1536, 1536], P('req'), may hold values from -0.15625 to 0.15625
- q_gain: float32 [1536], replicated, may hold values from 0 to 2
- k_gain: float32 [1536], replicated, may hold values from 0 to 2
- w_head: bfloat16 [1536, 64], replicated, may hold values from -0.15625 to 0.15625
- lengths: int32 [16], P('req'), may hold values from 288 to 2304, as said below
- guidance: float32 [16], P('req'), may hold values from 3 to 7
- step_size: float32 [16], P('req'), may hold values from 0.03 to 0.3
Outputs:
- new_latent: float32 [16, 2304, 64], P('req', 'seq', 'cfg')
Inputs may be any that keep to these rules, and one draw needn't show every extreme that they name: `lengths`: some request has exactly 2304 video tokens in every draw.
All inputs are finite; a program needn't handle non-finite values.
Results may differ from a plain program's by a relative error of at most 0.01.
Values may be sent and summed in bfloat16 or wider, within the bound.
A program may use at most 128 MiB of HBM per device.

v0:
```python
import jax
import jax.numpy as jnp
from jax import lax
from jax.sharding import PartitionSpec as P

DH = 128


def passed_along(value, axis, steps):
    count = lax.axis_size(axis)
    pairs = [(source, (source + steps) % count) for source in range(count)]
    return lax.ppermute(value, axis, pairs)


def from_partner(value, axis, apart):
    mask = 2**apart
    pairs = [(source, source ^ mask) for source in range(lax.axis_size(axis))]
    return lax.ppermute(value, axis, pairs)


def layer_norm(values):
    centered = values - jnp.mean(values, axis=-1, keepdims=True)
    return centered / jnp.sqrt(jnp.mean(centered * centered, axis=-1, keepdims=True) + 1e-06)


def rms_gain(values, gain):
    return values / jnp.sqrt(jnp.mean(values * values, axis=-1, keepdims=True) + 1e-06) * gain


def add_rows(left, piece):
    return jnp.dot(left, piece, preferred_element_type=jnp.float32)


def attend(state, query, stacked, start, length):
    top, total, weighted = state
    keys = stacked[0]
    values = stacked[1]
    count = keys.shape[0]
    scores = jnp.einsum("qhd,khd->qhk", query, keys, preferred_element_type=jnp.float32) / jnp.sqrt(
        jnp.float32(query.shape[2])
    )
    valid = start + jnp.arange(count, dtype=jnp.int32) < length
    scores = jnp.where(valid[None, None, :], scores, jnp.float32(-1e30))
    new_top = jnp.maximum(top, jnp.max(scores, axis=-1))
    factor = jnp.exp(top - new_top)
    probs = jnp.where(valid[None, None, :], jnp.exp(scores - new_top[:, :, None]), jnp.float32(0.0))
    total = total * factor + jnp.sum(probs, axis=-1)
    weighted = weighted * factor[:, :, None] + jnp.einsum(
        "qhk,khd->qhd", probs.astype(jnp.bfloat16), values, preferred_element_type=jnp.float32
    )
    return (new_top, total, weighted)


def local(
    hidden, latent, modulation, w_qkv, w_out, q_gain, k_gain, w_head, lengths, guidance, step_size
):
    state = hidden[0, 0]
    modes = modulation[0]
    length = lengths[0]
    rows = state.shape[0]
    width = state.shape[1]
    heads = q_gain.shape[0] // DH
    wide = state.astype(jnp.float32)
    normed = (layer_norm(wide) * (1.0 + modes[1]) + modes[0]).astype(jnp.bfloat16)
    qkv = add_rows(normed, lax.all_gather(w_qkv, "req", axis=0, tiled=True))
    query = rms_gain(qkv[:, :width], q_gain).astype(jnp.bfloat16).reshape(rows, heads, DH)
    keys = rms_gain(qkv[:, width : 2 * width], k_gain).astype(jnp.bfloat16).reshape(rows, heads, DH)
    values = qkv[:, 2 * width :].astype(jnp.bfloat16).reshape(rows, heads, DH)
    stacked = jnp.stack([keys, values])
    position = lax.axis_index("seq")
    members = lax.axis_size("seq")
    start_state = (
        jnp.full((rows, heads), -1e30, jnp.float32),
        jnp.zeros((rows, heads), jnp.float32),
        jnp.zeros((rows, heads, DH), jnp.float32),
    )
    first = attend(start_state, query, stacked, position * rows, length)

    def cycle_step(turn, carry):
        moving, inner = carry
        moving = passed_along(moving, "seq", 1)
        source = (position - turn) % members
        return (moving, attend(inner, query, moving, source * rows, length))

    moved, result = lax.fori_loop(1, members, cycle_step, (stacked, first))
    top, total, weighted = result
    attended = (weighted / total[:, :, None]).reshape(rows, width).astype(jnp.bfloat16)
    projected = add_rows(attended, lax.all_gather(w_out, "req", axis=0, tiled=True))
    block_out = (wide + modes[2] * projected).astype(jnp.bfloat16)
    head_in = (layer_norm(block_out.astype(jnp.float32)) * (1.0 + modes[4]) + modes[3]).astype(
        jnp.bfloat16
    )
    velocity = jnp.dot(head_in, w_head, preferred_element_type=jnp.float32)
    branch = lax.axis_index("cfg")
    scale = guidance[0]
    channels = velocity.shape[1] // 2
    own = lax.dynamic_slice_in_dim(velocity, branch * channels, channels, 1)
    outgoing = lax.dynamic_slice_in_dim(velocity, (1 - branch) * channels, channels, 1)
    other = from_partner(outgoing.astype(jnp.bfloat16), "cfg", 0).astype(outgoing.dtype)
    cond = jnp.where(branch == 0, own, other)
    uncond = jnp.where(branch == 0, other, own)
    guided = uncond + scale * (cond - uncond)
    valid = position * rows + jnp.arange(rows, dtype=jnp.int32) < length
    current = latent[0]
    updated = jnp.where(valid[:, None], current - step_size[0] * guided, current)
    return updated[None]


def solution(mesh):
    return jax.shard_map(
        local,
        mesh=mesh,
        in_specs=(
            P("cfg", "req", "seq", None),
            P("req", "seq", "cfg"),
            P("req", None, None),
            P("req", None),
            P("req", None),
            P(),
            P(),
            P(),
            P("req"),
            P("req"),
            P("req"),
        ),
        out_specs=P("req", "seq", "cfg"),
        check_vma=False,
    )
```

profile of v0, /device:TPU:1, one launch (start us, length us, event | category | flops | bytes accessed | tf_op | source)
XLA Modules:
  0.0 648.4 jit_solution(9502393456810084686)
XLA Ops:
  10.2 198.2 %all-gather.3.cloned.1.call-done = bf16[1536,4608]{1,0:T(8,128)(2,1)} async-done(((bf16[96,4608]{1,0:T(8,128)(2,1)}), bf16[1536,4608]{1,0:T(8,128)(2,1)}) %all-gather.3.cloned.1.call-update) | async-done | bytes 14155792 | tf_op jit(solution)/shard_map/all_gather | solution.py:65
  208.3 7.9 %fusion.42 = f32[288,4608]{1,0:T(8,128)S(1)} fusion(bf16[1536,4608]{1,0:T(8,128)(2,1)} %all-gather.3.cloned.1.call-done, bf16[1,1,288,1536]{3,2,1,0:T(8,128)(2,1)S(1)} %copy-done.2, f32[1536]{0:T(1024)S(1)} %get-tuple-element.226, f32[1536]{0:T(1024)S(1)} %get-tuple-element.227, f32[288]{0:T(512)S(1)} %add_sqrt_fusion.3, f32[288]{0:T(512)S(1)} %broadcast_multiply_fusion.1), kind=kOutput, calls=%fused_computation.61 | convolution fusion | flops 4079517696 | bytes 20363520 | tf_op jit(solution)/shard_map/dot_general | solution.py:31
  216.7 1.9 copy-done.1
  218.6 1.5 fusion.56
  220.1 1.0 copy-done.4
  222.8 1.7 copy.25
  226.7 1.5 fusion.21
  228.2 5.1 bitcast_add_fusion.1
  233.3 75.5 %all-gather.5.cloned.1.call-done = bf16[1536,1536]{1,0:T(8,128)(2,1)} async-done(((bf16[96,1536]{1,0:T(8,128)(2,1)}), bf16[1536,1536]{1,0:T(8,128)(2,1)}) %all-gather.5.cloned.1.call-update) | async-done | bytes 4718608 | tf_op jit(solution)/shard_map/all_gather | solution.py:88
  308.7 315.1 %while.21 = (s32[]{:T(128)}, bf16[2,288,12,128]{3,1,2,0:T(8,128)(2,1)}, f32[288,12]{0,1:T(8,128)S(1)}, f32[288,12]{0,1:T(8,128)S(1)}, f32[288,12,128]{2,0,1:T(8,...) while((s32[]{:T(128)}, ...), condition=%wide.region_9.10_spmd, body=%wide.region_6.9_spmd.sunk | while | flops 523439424 | bytes 44481960 | solution.py:85
  308.7 1.2 collective-permute-start
  310.6 36.8 %collective-permute-done = bf16[2,288,12,128]{3,1,2,0:T(8,128)(2,1)S(1)} collective-permute-done((bf16[2,288,12,128]{3,1,2,0:T(8,128)(2,1)}, bf16[2,288,12,128]{3,1,2,0:T(8,128)(2,1)S(1)}, u32[]{:S(2)}, u32[]{:S(2)}) %collective-permute-start) | collective-permute-done | bytes 1769504 | tf_op jit(solution)/shard_map/while/body/eval_jaxpr/ppermute | solution.py:12
  348.3 1.5 fusion.80
  349.8 1.3 copy.66
  351.9 3.1 bitcast_add_fusion.3
  355.0 1.3 copy-done.10
  357.0 37.1 %collective-permute-done = bf16[2,288,12,128]{3,1,2,0:T(8,128)(2,1)S(1)} collective-permute-done((bf16[2,288,12,128]{3,1,2,0:T(8,128)(2,1)}, bf16[2,288,12,128]{3,1,2,0:T(8,128)(2,1)S(1)}, u32[]{:S(2)}, u32[]{:S(2)}) %collective-permute-start) | collective-permute-done | bytes 1769504 | tf_op jit(solution)/shard_map/while/body/eval_jaxpr/ppermute | solution.py:12
  395.1 1.5 fusion.80
  396.6 1.3 copy.66
  398.7 3.1 bitcast_add_fusion.3
  401.8 1.3 copy-done.10
  403.7 36.3 %collective-permute-done = bf16[2,288,12,128]{3,1,2,0:T(8,128)(2,1)S(1)} collective-permute-done((bf16[2,288,12,128]{3,1,2,0:T(8,128)(2,1)}, bf16[2,288,12,128]{3,1,2,0:T(8,128)(2,1)S(1)}, u32[]{:S(2)}, u32[]{:S(2)}) %collective-permute-start) | collective-permute-done | bytes 1769504 | tf_op jit(solution)/shard_map/while/body/eval_jaxpr/ppermute | solution.py:12
  440.9 1.5 fusion.80
  442.4 1.3 copy.66
  444.6 3.1 bitcast_add_fusion.3
  447.6 1.3 copy-done.10
  449.6 35.4 %collective-permute-done = bf16[2,288,12,128]{3,1,2,0:T(8,128)(2,1)S(1)} collective-permute-done((bf16[2,288,12,128]{3,1,2,0:T(8,128)(2,1)}, bf16[2,288,12,128]{3,1,2,0:T(8,128)(2,1)S(1)}, u32[]{:S(2)}, u32[]{:S(2)}) %collective-permute-start) | collective-permute-done | bytes 1769504 | tf_op jit(solution)/shard_map/while/body/eval_jaxpr/ppermute | solution.py:12
  485.9 1.5 fusion.80
  487.5 1.3 copy.66
  489.6 3.1 bitcast_add_fusion.3
  492.6 1.3 copy-done.10
  494.6 34.5 %collective-permute-done = bf16[2,288,12,128]{3,1,2,0:T(8,128)(2,1)S(1)} collective-permute-done((bf16[2,288,12,128]{3,1,2,0:T(8,128)(2,1)}, bf16[2,288,12,128]{3,1,2,0:T(8,128)(2,1)S(1)}, u32[]{:S(2)}, u32[]{:S(2)}) %collective-permute-start) | collective-permute-done | bytes 1769504 | tf_op jit(solution)/shard_map/while/body/eval_jaxpr/ppermute | solution.py:12
  530.1 1.5 fusion.80
  531.6 1.3 copy.66
  533.7 3.1 bitcast_add_fusion.3
  536.8 1.3 copy-done.10
  538.8 33.7 %collective-permute-done = bf16[2,288,12,128]{3,1,2,0:T(8,128)(2,1)S(1)} collective-permute-done((bf16[2,288,12,128]{3,1,2,0:T(8,128)(2,1)}, bf16[2,288,12,128]{3,1,2,0:T(8,128)(2,1)S(1)}, u32[]{:S(2)}, u32[]{:S(2)}) %collective-permute-start) | collective-permute-done | bytes 1769504 | tf_op jit(solution)/shard_map/while/body/eval_jaxpr/ppermute | solution.py:12
  573.4 1.5 fusion.80
  574.9 1.3 copy.66
  577.0 3.1 bitcast_add_fusion.3
  580.1 1.3 copy-done.10
  582.1 32.8 %collective-permute-done = bf16[2,288,12,128]{3,1,2,0:T(8,128)(2,1)S(1)} collective-permute-done((bf16[2,288,12,128]{3,1,2,0:T(8,128)(2,1)}, bf16[2,288,12,128]{3,1,2,0:T(8,128)(2,1)S(1)}, u32[]{:S(2)}, u32[]{:S(2)}) %collective-permute-start) | collective-permute-done | bytes 1769504 | tf_op jit(solution)/shard_map/while/body/eval_jaxpr/ppermute | solution.py:12
  615.9 1.5 fusion.80
  617.4 1.3 copy.66
  619.5 3.1 bitcast_add_fusion.3
  622.6 1.3 copy-done.10
  623.8 4.8 fusion.67
  629.6 9.9 %collective-permute-start.1 = (bf16[288,32]{0,1:T(8,128)(2,1)S(1)}, bf16[288,32]{0,1:T(8,128)(2,1)S(1)}, u32[]{:S(2)}, u32[]{:S(2)}) collective-permute-start(bf16[288,32]{0,1:T(8,128)(2,1)S(1)} %dynamic-slice_convert_fusion), channel_id=1, source_target_pairs={{0,128},{128,0},{1,129},{129,1},{2,130},{130,2},{3,131},{131,3},{4... | collective-permute-start | bytes 55304 | tf_op jit(solution)/shard_map/ppermute | solution.py:18
  (105 shorter events, 26.1 us)
Async XLA Ops:
  6.5 622.5 %copy-start = (bf16[1536,64]{0,1:T(8,128)(2,1)S(1)}, bf16[1536,64]{0,1:T(8,128)(2,1)}, u32[]{:S(2)}) copy-start(bf16[1536,64]{0,1:T(8,128)(2,1)} %param.20) | copy-start | bytes 589828
  6.5 3.0 copy-start.2
  6.5 201.8 %all-gather.3.cloned.1.call-start = ((), (), s32[]{:S(2)}) async-start(), calls=%async_computation | async-start | bytes 15040512 | tf_op jit(solution)/shard_map/all_gather | solution.py:65
  7.3 301.5 %all-gather.5.cloned.1.call-start = ((), (), s32[]{:S(2)}) async-start(), calls=%async_computation.1 | async-start | bytes 5013504 | tf_op jit(solution)/shard_map/all_gather | solution.py:88
  216.2 2.3 copy-start.1
  216.4 2.2 copy-start.7
  216.4 2.2 copy-start.8
  220.1 1.0 copy-start.4
  222.8 1.7 copy-start.3
  224.5 1.2 copy-start.5
  308.7 38.6 %collective-permute-start = (bf16[2,288,12,128]{3,1,2,0:T(8,128)(2,1)}, bf16[2,288,12,128]{3,1,2,0:T(8,128)(2,1)S(1)}, u32[]{:S(2)}, u32[]{:S(2)}) collective-permute-start(bf16[2,288,12,128]{3,1,2,0:T(8,128)(2,1)} %get-tuple-element.331), channel_id=1, source_target_pairs={{0,1},{1,2},{2,3},{3,4},{4,5},{5,6},{6,7},{7,0},{8,9},{9,10},{10,1... | collective-permute-start | bytes 5308424 | tf_op jit(solution)/shard_map/while/body/eval_jaxpr/ppermute | solution.py:12
  349.8 2.1 copy-start.9
  355.0 1.3 copy-start.10
  356.3 37.8 %collective-permute-start = (bf16[2,288,12,128]{3,1,2,0:T(8,128)(2,1)}, bf16[2,288,12,128]{3,1,2,0:T(8,128)(2,1)S(1)}, u32[]{:S(2)}, u32[]{:S(2)}) collective-permute-start(bf16[2,288,12,128]{3,1,2,0:T(8,128)(2,1)} %get-tuple-element.331), channel_id=1, source_target_pairs={{0,1},{1,2},{2,3},{3,4},{4,5},{5,6},{6,7},{7,0},{8,9},{9,10},{10,1... | collective-permute-start | bytes 5308424 | tf_op jit(solution)/shard_map/while/body/eval_jaxpr/ppermute | solution.py:12
  396.6 2.1 copy-start.9
  401.8 1.3 copy-start.10
  403.0 36.9 %collective-permute-start = (bf16[2,288,12,128]{3,1,2,0:T(8,128)(2,1)}, bf16[2,288,12,128]{3,1,2,0:T(8,128)(2,1)S(1)}, u32[]{:S(2)}, u32[]{:S(2)}) collective-permute-start(bf16[2,288,12,128]{3,1,2,0:T(8,128)(2,1)} %get-tuple-element.331), channel_id=1, source_target_pairs={{0,1},{1,2},{2,3},{3,4},{4,5},{5,6},{6,7},{7,0},{8,9},{9,10},{10,1... | collective-permute-start | bytes 5308424 | tf_op jit(solution)/shard_map/while/body/eval_jaxpr/ppermute | solution.py:12
  442.4 2.1 copy-start.9
  447.6 1.3 copy-start.10
  448.9 36.0 %collective-permute-start = (bf16[2,288,12,128]{3,1,2,0:T(8,128)(2,1)}, bf16[2,288,12,128]{3,1,2,0:T(8,128)(2,1)S(1)}, u32[]{:S(2)}, u32[]{:S(2)}) collective-permute-start(bf16[2,288,12,128]{3,1,2,0:T(8,128)(2,1)} %get-tuple-element.331), channel_id=1, source_target_pairs={{0,1},{1,2},{2,3},{3,4},{4,5},{5,6},{6,7},{7,0},{8,9},{9,10},{10,1... | collective-permute-start | bytes 5308424 | tf_op jit(solution)/shard_map/while/body/eval_jaxpr/ppermute | solution.py:12
  487.5 2.1 copy-start.9
  492.6 1.3 copy-start.10
  493.9 35.2 %collective-permute-start = (bf16[2,288,12,128]{3,1,2,0:T(8,128)(2,1)}, bf16[2,288,12,128]{3,1,2,0:T(8,128)(2,1)S(1)}, u32[]{:S(2)}, u32[]{:S(2)}) collective-permute-start(bf16[2,288,12,128]{3,1,2,0:T(8,128)(2,1)} %get-tuple-element.331), channel_id=1, source_target_pairs={{0,1},{1,2},{2,3},{3,4},{4,5},{5,6},{6,7},{7,0},{8,9},{9,10},{10,1... | collective-permute-start | bytes 5308424 | tf_op jit(solution)/shard_map/while/body/eval_jaxpr/ppermute | solution.py:12
  531.6 2.1 copy-start.9
  536.8 1.3 copy-start.10
  538.1 34.3 %collective-permute-start = (bf16[2,288,12,128]{3,1,2,0:T(8,128)(2,1)}, bf16[2,288,12,128]{3,1,2,0:T(8,128)(2,1)S(1)}, u32[]{:S(2)}, u32[]{:S(2)}) collective-permute-start(bf16[2,288,12,128]{3,1,2,0:T(8,128)(2,1)} %get-tuple-element.331), channel_id=1, source_target_pairs={{0,1},{1,2},{2,3},{3,4},{4,5},{5,6},{6,7},{7,0},{8,9},{9,10},{10,1... | collective-permute-start | bytes 5308424 | tf_op jit(solution)/shard_map/while/body/eval_jaxpr/ppermute | solution.py:12
  574.9 2.1 copy-start.9
  580.1 1.3 copy-start.10
  581.4 33.5 %collective-permute-start = (bf16[2,288,12,128]{3,1,2,0:T(8,128)(2,1)}, bf16[2,288,12,128]{3,1,2,0:T(8,128)(2,1)S(1)}, u32[]{:S(2)}, u32[]{:S(2)}) collective-permute-start(bf16[2,288,12,128]{3,1,2,0:T(8,128)(2,1)} %get-tuple-element.331), channel_id=1, source_target_pairs={{0,1},{1,2},{2,3},{3,4},{4,5},{5,6},{6,7},{7,0},{8,9},{9,10},{10,1... | collective-permute-start | bytes 5308424 | tf_op jit(solution)/shard_map/while/body/eval_jaxpr/ppermute | solution.py:12
  617.4 2.1 copy-start.9
  622.6 1.3 copy-start.10
  629.0 11.8 %copy-start.6 = (f32[1,288,32]{1,2,0:T(8,128)S(1)}, f32[1,288,32]{1,2,0:T(8,128)}, u32[]{:S(2)}) copy-start(f32[1,288,32]{1,2,0:T(8,128)} %param.14) | copy-start | bytes 110596
  629.6 11.2 %collective-permute-start.1 = (bf16[288,32]{0,1:T(8,128)(2,1)S(1)}, bf16[288,32]{0,1:T(8,128)(2,1)S(1)}, u32[]{:S(2)}, u32[]{:S(2)}) collective-permute-start(bf16[288,32]{0,1:T(8,128)(2,1)S(1)} %dynamic-slice_convert_fusion), channel_id=1, source_target_pairs={{0,128},{128,0},{1,129},{129,1},{2,130},{130,2},{3,131},{131,3},{4... | collective-permute-start | bytes 55304 | tf_op jit(solution)/shard_map/ppermute | solution.py:18
Sparse Core Ops, SparseCore 0:
  9.9 198.3 all-gather.2
  210.9 97.7 all-gather.4
where the time goes:
time: 649 us; the launch traced here: 648 us
  waiting for transfers between devices  522 us (80%)
  matrix products  47.4 us (7%)
  local copies, waits for them, and re-layouts  30.9 us (5%)
  other arithmetic  21.2 us (3%)
  between operations  15.5 us (2%)
  starting transfers between devices  11.2 us (2%)
    ppermute x7, waiting for transfers between devices, passed_along(): return lax.ppermute(value, axis, pairs)  247 us
    all_gather x1, waiting for transfers between devices, local(): qkv = add_rows(normed, lax.all_gather(w_qkv, 'req', axis=0, tiled=True))  198 us
    all_gather x1, waiting for transfers between devices, local(): lax.all_gather(w_out, 'req', axis=0, tiled=True)  75.5 us
    dot_general x8, matrix products, attend(): jnp.einsum('qhk,khd->qhd', probs.astype(jnp.bfloat16), values, preferred_...  26.5 us
    while x42, local copies, waits for them, and re-layouts  23.8 us
  transfers between devices with their start and end apart: 10, of which 9 were waited for; matrix products, arithmetic and copies ran while one was open for 4% of the time, Pallas kernels for 0%

commit v1 on v0

v1 whole, which is shorter than its diff:
```python
import functools
import math

import jax
import jax.numpy as jnp
from jax import lax
from jax.experimental import pallas as pl
from jax.experimental.pallas import tpu as pltpu
from jax.sharding import PartitionSpec as P

MESH = pl.DeviceIdType.MESH
DH = 128
NY = 4
EPS = 1e-6
CH = 48


def norm_rows(x, scale, shift):
    c = x - jnp.mean(x, axis=-1, keepdims=True)
    return c * lax.rsqrt(jnp.mean(c * c, axis=-1, keepdims=True) + EPS) * (1.0 + scale) + shift


def kernel(
    NX,
    NZ,
    hid,
    wqkv,
    wout,
    mod,
    qg,
    kg,
    whead,
    length,
    guid,
    out,
    X,
    W,
    WO,
    xn,
    qk32,
    ssb,
    qbuf,
    kbuf,
    vbuf,
    att_s,
    att_r,
    acc,
    vsend,
    vrecv,
    bias,
    x_recv,
    t_send,
    y_send,
    w_recv,
    ring_send,
    share_send,
    xe_send,
    loc_sem,
    ss_send,
    ss_recv,
    kv_send,
    kv_recv,
    at_send,
    at_recv,
    v_send,
    v_recv,
):
    rows, width = hid.shape
    G = width // NY
    heads = G // DH
    HR = rows // 2
    R = NX * NZ
    half = NZ // 2
    k = lax.axis_index("cfg")
    r = lax.axis_index("req")
    s = lax.axis_index("seq")
    xh, z = r // NZ, r % NZ
    p, y = s // NY, s % NY

    def seq_of(a, b):
        return a * NY + b % NY

    yp = (k, r, seq_of(p, y + 1))
    ym = (k, r, seq_of(p, y + 3))
    y2 = (k, r, seq_of(p, y + 2))
    transposed = (p, r, k * NY + y)
    partner = (1 - k, r, s)
    xpart = (k, (1 - xh) * NZ + z, s)
    znext = (k, xh * NZ + (z + 1 + k * (NZ - 2)) % NZ, s)

    def remote(src, dst, ssem, rsem, dev):
        return pltpu.make_async_remote_copy(
            src_ref=src, dst_ref=dst, send_sem=ssem, recv_sem=rsem, device_id=dev, device_id_type=MESH
        )

    loc_w = [
        pltpu.make_async_copy(
            wqkv.at[:, pl.ds(pl.multiple_of(j * width + y * G, G), G)],
            W.at[r, :, pl.ds(j * G, G)],
            loc_sem.at[j],
        )
        for j in range(3)
    ]
    loc_wo = pltpu.make_async_copy(wout, WO.at[r], loc_sem.at[3])
    for c in loc_w:
        c.start()
    loc_wo.start()

    def hrows(h):
        return pl.ds(h * HR, HR)

    @pl.when(k == p)
    def _():
        for h in range(2):
            pltpu.make_async_copy(hid.at[hrows(h)], X.at[y, hrows(h)], x_recv.at[y, h]).start()

    barrier = pltpu.get_barrier_semaphore()
    peers = [
        yp,
        ym,
        y2,
        partner,
        (k, r, (1 - p) * NY + y),
        (1 - k, r, (1 - p) * NY + y),
    ]
    if NX > 1:
        peers.append(xpart)
    if NZ > 1:
        peers.append((k, xh * NZ + (z + 1) % NZ, s))
        peers.append((k, xh * NZ + (z + NZ - 1) % NZ, s))
    for dev in peers:
        pl.semaphore_signal(barrier, inc=1, device_id=dev, device_id_type=MESH)
    pl.semaphore_wait(barrier, len(peers))

    t_copies = [
        remote(hid.at[hrows(h)], X.at[y, hrows(h)], t_send.at[h], x_recv.at[y, h], transposed) for h in range(2)
    ]

    @pl.when(k != p)
    def _():
        for c in t_copies:
            c.start()

    bufs = (W, WO)

    def slot_at(side, t):
        other = xh if side == 0 else 1 - xh
        return other * NZ + (z + t * (NZ - 1) + k * 2 * t) % NZ

    def ring_copy(m, side, t):
        j = slot_at(side, t)
        return remote(bufs[m].at[j], bufs[m].at[j], ring_send.at[m, side, t], w_recv.at[m, j], znext)

    def share_copy(m, side, t):
        j = slot_at(side, t)
        return remote(bufs[m].at[j], bufs[m].at[j], share_send.at[m, side, t - 1], w_recv.at[m, j], partner)

    def mine(side):
        return (xh if side == 0 else 1 - xh) == k

    def recv_wait(m, j):
        pltpu.make_async_copy(bufs[m].at[j], bufs[m].at[j], w_recv.at[m, j]).wait()

    def ring_start(m, side):
        if NZ > 1:
            if half > 1:
                ring_copy(m, side, 0).start()
            else:

                @pl.when(mine(side))
                def _():
                    ring_copy(m, side, 0).start()

    def xe_copy(m):
        return remote(bufs[m].at[r], bufs[m].at[r], xe_send.at[m], w_recv.at[m, r], xpart)

    def ring_open(m):
        ring_start(m, 0)
        if NX > 1:
            xe_copy(m).start()

    def ring_second(m):
        if NX > 1:
            recv_wait(m, (1 - xh) * NZ + z)
            ring_start(m, 1)

    def ring_step(m, side, t):
        if NZ == 1 or t > half or side >= NX:
            return

        def go():
            recv_wait(m, slot_at(side, t))
            if t < half - 1:
                ring_copy(m, side, t).start()
            elif t == half - 1:

                @pl.when(mine(side))
                def _():
                    ring_copy(m, side, t).start()

            share_copy(m, side, t).start()

        if t < half:
            go()
        else:
            pl.when(mine(side))(go)

    def ring_shared(m):
        for side in range(NX):
            for t in range(half + 1, NZ):
                recv_wait(m, slot_at(side, t))
            if NZ > 1:

                @pl.when(jnp.logical_not(mine(side)))
                def _():
                    recv_wait(m, slot_at(side, half))

    def ring_drain(m):
        if NX > 1:
            xe_copy(m).wait_send()
        for side in range(NX):
            for t in range(half):
                if t < half - 1:
                    ring_copy(m, side, t).wait_send()
                else:

                    @pl.when(mine(side))
                    def _():
                        ring_copy(m, side, t).wait_send()

            for t in range(1, half + 1):
                if t < half:
                    share_copy(m, side, t).wait_send()
                else:

                    @pl.when(mine(side))
                    def _():
                        share_copy(m, side, t).wait_send()

    def x_copy(slot, h, n, dev):
        return remote(X.at[slot, hrows(h)], X.at[slot, hrows(h)], y_send.at[n], x_recv.at[slot, h], dev)

    def x_wait(slot, h):
        pltpu.make_async_copy(X.at[slot, hrows(h)], X.at[slot, hrows(h)], x_recv.at[slot, h]).wait()

    below, above, across = (y + 3) % NY, (y + 1) % NY, (y + 2) % NY
    x_sends = [
        x_copy(y, 0, 0, yp),
        x_copy(y, 1, 1, ym),
        x_copy(y, 1, 2, yp),
        x_copy(y, 0, 3, ym),
        x_copy(below, 0, 4, yp),
        x_copy(above, 1, 5, ym),
    ]

    def layer_in(slot):
        def chunk(i, carry):
            at = pl.ds(pl.multiple_of(i * CH, CH), CH)
            x = X[slot, at, :].astype(jnp.float32)
            xn[at, :] = norm_rows(x, mod[1:2, :], mod[0:1, :]).astype(jnp.bfloat16)
            return carry

        lax.fori_loop(0, rows // CH, chunk, 0)

    lanes = lax.broadcasted_iota(jnp.int32, (rows, DH), 1)

    def project(slot):
        qkv = jnp.dot(xn[...], W[...].reshape(width, 3 * G), preferred_element_type=jnp.float32)
        q = qkv[:, :G]
        kk = qkv[:, G : 2 * G]
        qk32[slot] = qkv[:, : 2 * G]
        sq = jnp.sum(q * q, axis=1, keepdims=True)
        sk = jnp.sum(kk * kk, axis=1, keepdims=True)
        both = jnp.where(lanes == 0, sq, jnp.where(lanes == 1, sk, 0.0))
        both = jnp.concatenate([both, jnp.zeros((G - rows, DH), jnp.float32)], axis=0)
        ssb[y, slot] = both.T[:8, :]
        for h in range(heads):
            vbuf[h, k * NY + slot] = qkv[:, 2 * G + h * DH : 2 * G + (h + 1) * DH].astype(jnp.bfloat16)

    def ss_copies(slot):
        return [
            remote(ssb.at[y, slot], ssb.at[y, slot], ss_send.at[n, slot], ss_recv.at[y, slot], dev)
            for n, dev in enumerate((y2, yp, ym))
        ]

    def kv_copy(which, slot):
        buf = (kbuf, vbuf)[which]
        at = k * NY + slot
        return remote(buf.at[:, at], buf.at[:, at], kv_send.at[which, slot], kv_recv.at[which, at], partner)

    def kv_wait(which, at):
        buf = (kbuf, vbuf)[which]
        pltpu.make_async_copy(buf.at[:, at], buf.at[:, at], kv_recv.at[which, at]).wait()

    position = lax.broadcasted_iota(jnp.int32, (8, 2 * NY * rows), 1)
    bias[...] = jnp.where(position < length[0], 0.0, -1e30)
    for c in loc_w:
        c.wait()
    ring_open(0)
    x_wait(y, 0)
    x_sends[0].start()
    ring_step(0, 0, 1)
    ring_second(0)
    ring_step(0, 0, 2)
    x_wait(y, 1)
    for c in x_sends[1:4]:
        c.start()
    ring_step(0, 1, 1)
    ring_step(0, 0, 3)
    layer_in(y)
    ring_step(0, 1, 2)
    ring_step(0, 0, 4)
    x_wait(below, 0)
    x_sends[4].start()
    x_wait(above, 1)
    x_sends[5].start()
    ring_step(0, 1, 3)
    ring_step(0, 1, 4)
    loc_wo.wait()
    ring_open(1)
    ring_shared(0)

    order = (y, below, above, across)
    for i, slot in enumerate(order):
        if i > 0:
            if i == 1:
                x_wait(below, 1)
            elif i == 2:
                x_wait(above, 0)
            else:
                x_wait(across, 0)
                x_wait(across, 1)
            layer_in(slot)
        project(slot)
        for c in ss_copies(slot):
            c.start()
        kv_copy(1, slot).start()
        if i == 0:
            ring_second(1)
        elif i == 1:
            ring_step(1, 0, 1)
        elif i == 2:
            ring_step(1, 1, 1)

    factor = math.log2(math.e) / math.sqrt(DH)
    cols = pl.ds(pl.multiple_of(y * G, G), G)
    qgain = qg[:, cols] * factor
    kgain = kg[:, cols]

    def finish(slot, which):
        total = ssb[0, slot] + ssb[1, slot] + ssb[2, slot] + ssb[3, slot]
        inv = lax.rsqrt(total * (1.0 / width) + EPS)
        inv = jnp.concatenate([inv, jnp.zeros((DH - 8, G), jnp.float32)], axis=0).T
        q = (qk32[slot, :, :G] * inv[:rows, 0:1] * qgain).astype(jnp.bfloat16)
        kk = (qk32[slot, :, G:] * inv[:rows, 1:2] * kgain).astype(jnp.bfloat16)
        for h in range(heads):
            kbuf[h, k * NY + slot] = kk[:, h * DH : (h + 1) * DH]
            qbuf[slot, h] = q[:, h * DH : (h + 1) * DH]

    for slot in order:
        for src in (below, above, across):
            pltpu.make_async_copy(ssb.at[src, slot], ssb.at[src, slot], ss_recv.at[src, slot]).wait()
        finish(slot, 0)
        kv_copy(0, slot).start()
    ring_step(1, 0, 2)
    ring_step(1, 1, 2)
    for which in (1, 0):
        for slot in range(NY):
            kv_wait(which, (1 - k) * NY + slot)

    keys = 2 * NY * rows

    def attend(slot, h):
        q = qbuf[slot, h]
        sc = lax.dot_general(
            q, kbuf[h].reshape(keys, DH), (((1,), (1,)), ((), ())), preferred_element_type=jnp.float32
        )
        sc = sc + bias[0:1, :]
        top = jnp.max(sc, axis=1, keepdims=True)
        pr = jnp.exp2(sc - top)
        total = jnp.sum(pr, axis=1, keepdims=True)
        o = jnp.dot(pr.astype(jnp.bfloat16), vbuf[h].reshape(keys, DH), preferred_element_type=jnp.float32)
        att_s[slot, h] = (o / total).astype(jnp.bfloat16)

    def at_copy(n, slot, dev):
        return remote(att_s.at[slot], att_r.at[y], at_send.at[n], at_recv.at[y], dev)

    dests = ((across, y2), (above, yp), (below, ym), (y, None))

    for n, (slot, dev) in enumerate(dests):

        def head(h, carry, slot=slot):
            attend(slot, h)
            return carry

        lax.fori_loop(0, heads, head, 0)
        if dev is not None:
            at_copy(n, slot, dev).start()
        if n == 0:
            ring_step(1, 0, 3)
            ring_step(1, 1, 3)
        elif n == 1:
            ring_step(1, 0, 4)
            ring_step(1, 1, 4)

    ring_shared(1)
    per = R // NY if R >= NY else 1

    def out_rows(g):
        if R >= NY:
            return WO[pl.ds(g * per, per)].reshape(G, width)
        return WO[0, pl.ds(pl.multiple_of(g * G, G), G), :]

    def joined(ref, g):
        return jnp.concatenate([ref[g, h] for h in range(heads)], axis=1)

    acc[...] = jnp.dot(joined(att_s, y), out_rows(y), preferred_element_type=jnp.float32)
    for g in (above, below, across):
        pltpu.make_async_copy(att_r.at[g], att_r.at[g], at_recv.at[g]).wait()
        acc[...] += jnp.dot(joined(att_r, g), out_rows(g), preferred_element_type=jnp.float32)

    def tail(i, carry):
        at = pl.ds(pl.multiple_of(i * CH, CH), CH)
        x = X[y, at, :].astype(jnp.float32)
        b = (x + mod[2:3, :] * acc[at, :]).astype(jnp.bfloat16).astype(jnp.float32)
        xn[at, :] = norm_rows(b, mod[4:5, :], mod[3:4, :]).astype(jnp.bfloat16)
        return carry

    lax.fori_loop(0, rows // CH, tail, 0)
    vel = jnp.dot(xn[...], whead[...], preferred_element_type=jnp.float32).astype(jnp.bfloat16)
    C = vel.shape[1] // 2
    vsend[0, :, :C] = vel[:, :C]
    vsend[1, :, :C] = vel[:, C:]

    for c in range(2):
        here = jnp.logical_and(p == k, k == c)

        @pl.when(here)
        def _():
            pltpu.make_async_copy(vsend.at[c], vrecv.at[p], v_recv.at[p]).start()

        @pl.when(jnp.logical_not(here))
        def _():
            remote(vsend.at[c], vrecv.at[p], v_send.at[c], v_recv.at[p], (c, r, k * NY + y)).start()

    for q in range(2):
        pltpu.make_async_copy(vrecv.at[q], vrecv.at[q], v_recv.at[q]).wait()
    cond = vrecv[0, :, :C].astype(jnp.float32)
    uncond = vrecv[1, :, :C].astype(jnp.float32)
    out[...] = uncond + guid[0] * (cond - uncond)

    @pl.when(k != p)
    def _():
        for c in t_copies:
            c.wait_send()

    for c in x_sends:
        c.wait_send()
    for m in range(2):
        ring_drain(m)
    for slot in range(NY):
        for c in ss_copies(slot):
            c.wait_send()
        for which in range(2):
            kv_copy(which, slot).wait_send()
    for n, (slot, dev) in enumerate(dests):
        if dev is not None:
            at_copy(n, slot, dev).wait_send()
    for c in range(2):
        here = jnp.logical_and(p == k, k == c)

        @pl.when(jnp.logical_not(here))
        def _():
            remote(vsend.at[c], vrecv.at[p], v_send.at[c], v_recv.at[p], (c, r, k * NY + y)).wait_send()


def solution(mesh):
    R = mesh.shape["req"]
    NX = 2 if R > 1 else 1
    NZ = R // NX
    DMA = pltpu.SemaphoreType.DMA
    bf, f32 = jnp.bfloat16, jnp.float32

    def local(hidden, latent, modulation, w_qkv, w_out, q_gain, k_gain, w_head, lengths, guidance, step_size):
        rows, width = hidden.shape[2:]
        G = width // NY
        heads = G // DH
        wr = w_qkv.shape[0]
        half = max(NZ // 2, 1)
        chans = w_head.shape[1] // 2
        seq = 2 * NY
        vmem = pl.BlockSpec(memory_space=pltpu.VMEM)
        smem = pl.BlockSpec(memory_space=pltpu.SMEM)
        hbm = pl.BlockSpec(memory_space=pl.ANY)
        guided = pl.pallas_call(
            functools.partial(kernel, NX, NZ),
            out_shape=jax.ShapeDtypeStruct((rows, chans), f32),
            in_specs=[hbm, hbm, hbm, vmem, vmem, vmem, vmem, smem, smem],
            out_specs=vmem,
            scratch_shapes=[
                pltpu.VMEM((NY, rows, width), bf),
                pltpu.VMEM((R, wr, 3 * G), bf),
                pltpu.VMEM((R, wr, width), bf),
                pltpu.VMEM((rows, width), bf),
                pltpu.VMEM((NY, rows, 2 * G), f32),
                pltpu.VMEM((NY, NY, 8, G), f32),
                pltpu.VMEM((NY, heads, rows, DH), bf),
                pltpu.VMEM((heads, seq, rows, DH), bf),
                pltpu.VMEM((heads, seq, rows, DH), bf),
                pltpu.VMEM((NY, heads, rows, DH), bf),
                pltpu.VMEM((NY, heads, rows, DH), bf),
                pltpu.VMEM((rows, width), f32),
                pltpu.VMEM((2, rows, DH), bf),
                pltpu.VMEM((2, rows, DH), bf),
                pltpu.VMEM((8, seq * rows), f32),
                DMA((NY, 2)),
                DMA((2,)),
                DMA((6,)),
                DMA((2, R)),
                DMA((2, 2, half)),
                DMA((2, 2, half)),
                DMA((2,)),
                DMA((4,)),
                DMA((3, NY)),
                DMA((NY, NY)),
                DMA((2, NY)),
                DMA((2, seq)),
                DMA((4,)),
                DMA((NY,)),
                DMA((2,)),
                DMA((2,)),
            ],
            compiler_params=pltpu.CompilerParams(
                collective_id=0, has_side_effects=True, vmem_limit_bytes=60 * 1024 * 1024
            ),
            name="block",
        )(
            hidden[0, 0],
            w_qkv,
            w_out,
            modulation[0],
            q_gain[None],
            k_gain[None],
            w_head,
            lengths,
            guidance,
        )
        position = lax.axis_index("seq")
        valid = position * rows + jnp.arange(rows, dtype=jnp.int32) < lengths[0]
        current = latent[0]
        return jnp.where(valid[:, None], current - step_size[0] * guided, current)[None]

    return jax.shard_map(
        local,
        mesh=mesh,
        in_specs=(
            P("cfg", "req", "seq", None),
            P("req", "seq", "cfg"),
            P("req", None, None),
            P("req", None),
            P("req", None),
            P(),
            P(),
            P(),
            P("req"),
            P("req"),
            P("req"),
        ),
        out_specs=P("req", "seq", "cfg"),
        check_vma=False,
    )
```

time: 649 us -> 111 us (0.17)
  waiting for transfers between devices: 522 us -> 0 us
  Pallas kernels: 0 us -> 104 us
  matrix products: 47.4 us -> 0 us
  local copies, waits for them, and re-layouts: 30.9 us -> 4.72 us
  other arithmetic: 21.2 us -> 0.11 us
  between operations: 15.5 us -> 2.03 us
  starting transfers between devices: 11.2 us -> 0 us
    all_gather x2 -> x0, waiting for transfers between devices: 274 us -> none  [the longest x1 198 us: local(): qkv = add_rows(normed, lax.all_gather(w_qkv, 'req', axis=0, tiled=True))]
    ppermute x8 -> x0, waiting for transfers between devices: 247 us -> none  [the longest x7 247 us: passed_along(): return lax.ppermute(value, axis, pairs)]
    pallas_call x0 -> x1, Pallas kernels: none -> 104 us  [local(): pl.pallas_call(functools.partial(kernel, NX, NZ), out_shape=jax.ShapeDtyp...]
    dot_general x19 -> x0, matrix products: 47.4 us -> none  [the longest x8 26.5 us: attend(): jnp.einsum('qhk,khd->qhd', probs.astype(jnp.bfloat16), values, preferred_...]
    while x43 -> x0, local copies, waits for them, and re-layouts: 25.5 us -> none
    reduce_sum x12 -> x0, other arithmetic: 13 us -> none  [the longest x8 11.8 us: attend(): total = total * factor + jnp.sum(probs, axis=-1)]
    ppermute x8 -> x0, starting transfers between devices: 11.2 us -> none  [the longest x1 9.94 us: from_partner(): return lax.ppermute(value, axis, pairs)]
  transfers between devices with their start and end apart: 10 -> 0, of which waited for: 9 -> 0; matrix products, arithmetic and copies ran while one was open for 4% -> 0% of each run, Pallas kernels for 0% -> 0%
where the time goes in v1:
time: 111 us
  Pallas kernels  104 us (94%)
  local copies, waits for them, and re-layouts  4.72 us (4%)
  between operations  2.03 us (2%)
    pallas_call x1, Pallas kernels, local(): pl.pallas_call(functools.partial(kernel, NX, NZ), out_shape=jax.ShapeDtyp...  104 us
    unnamed x13, local copies, waits for them, and re-layouts  2.8 us

profile of v1, /device:TPU:1, one launch (start us, length us, event | category | flops | bytes accessed | tf_op | source)
XLA Modules:
  0.0 110.8 jit_solution(17552912271298820262)
XLA Ops:
  0.7 0.0 copy-start.2
  0.7 1.9 %copy.13.whead = bf16[1536,64]{1,0:T(8,128)(2,1)} copy(bf16[1536,64]{0,1:T(8,128)(2,1)} %param.18) | data formatting | bytes 393216 | tf_op args[7]
  2.5 0.0 copy-done.2
  2.5 0.0 copy-start.3
  2.5 0.6 copy.17
  3.1 0.0 copy-start.4
  3.1 0.1 copy-done.3
  3.2 0.6 broadcast_in_dim.19.qg
  3.8 0.0 copy-done.4
  3.8 0.6 broadcast_in_dim.20.kg
  5.1 0.0 copy-start.1
  5.1 103.9 %block.1 = f32[288,32]{1,0:T(8,128)} custom-call(bf16[288,1536]{1,0:T(8,128)(2,1)} %bitcast.12, bf16[96,4608]{1,0:T(8,128)(2,1)} %wqkv.1, bf16[96,1536]{1,0:T(8,128)(2,1)} %wout.1, f32[5,1536]{1,0:T(8,128)} %bitcast.13, f32[1,1536]{1,0:T(1,128)} %broadcast_in_dim.19.qg, f32[1,1536]{1,0:T(1,128)} %broadcast_in_dim.20.kg, bf16[1536,64]{1,0:T(8,128)(2,1)} %copy.13.whead, ...), custom_call_target="tpu_custom_call" | custom-call | tf_op jit(solution)/shard_map/block/pallas_call | solution.py:495
  109.0 0.0 copy-start
  109.1 0.0 copy-done.1
  109.1 0.1 copy.12
  109.8 0.1 copy-done
  109.9 0.1 fusion
  110.1 0.7 copy.14
  (1 shorter events, 0.0 us)
Async XLA Ops:
  0.7 1.9 %copy-start.2 = (f32[1,5,1536]{2,0,1:T(1,128)S(1)}, f32[1,5,1536]{2,0,1:T(1,128)}, u32[]{:S(2)}) copy-start(f32[1,5,1536]{2,0,1:T(1,128)} %param.13) | copy-start | bytes 92164
  2.5 0.7 copy-start.3
  3.1 0.7 copy-start.4
  5.1 104.0 %copy-start.1 = (f32[1,288,32]{1,2,0:T(8,128)S(1)}, f32[1,288,32]{1,2,0:T(8,128)}, u32[]{:S(2)}) copy-start(f32[1,288,32]{1,2,0:T(8,128)} %param.12) | copy-start | bytes 110596
  109.0 0.9 copy-start

commit v2 on v1

--- a/solution.py
+++ b/solution.py
@@ -32,6 +32,7 @@
     whead,
     length,
     guid,
+    step,
     out,
     X,
     W,
@@ -93,27 +94,6 @@
             src_ref=src, dst_ref=dst, send_sem=ssem, recv_sem=rsem, device_id=dev, device_id_type=MESH
         )
 
-    loc_w = [
-        pltpu.make_async_copy(
-            wqkv.at[:, pl.ds(pl.multiple_of(j * width + y * G, G), G)],
-            W.at[r, :, pl.ds(j * G, G)],
-            loc_sem.at[j],
-        )
-        for j in range(3)
-    ]
-    loc_wo = pltpu.make_async_copy(wout, WO.at[r], loc_sem.at[3])
-    for c in loc_w:
-        c.start()
-    loc_wo.start()
-
-    def hrows(h):
-        return pl.ds(h * HR, HR)
-
-    @pl.when(k == p)
-    def _():
-        for h in range(2):
-            pltpu.make_async_copy(hid.at[hrows(h)], X.at[y, hrows(h)], x_recv.at[y, h]).start()
-
     barrier = pltpu.get_barrier_semaphore()
     peers = [
         yp,
@@ -130,6 +110,27 @@
         peers.append((k, xh * NZ + (z + NZ - 1) % NZ, s))
     for dev in peers:
         pl.semaphore_signal(barrier, inc=1, device_id=dev, device_id_type=MESH)
+    loc_w = [
+        pltpu.make_async_copy(
+            wqkv.at[:, pl.ds(pl.multiple_of(j * width + y * G, G), G)],
+            W.at[r, :, pl.ds(j * G, G)],
+            loc_sem.at[j],
+        )
+        for j in range(3)
+    ]
+    loc_wo = pltpu.make_async_copy(wout, WO.at[r], loc_sem.at[3])
+    for c in loc_w:
+        c.start()
+    loc_wo.start()
+
+    def hrows(h):
+        return pl.ds(h * HR, HR)
+
+    @pl.when(k == p)
+    def _():
+        for h in range(2):
+            pltpu.make_async_copy(hid.at[hrows(h)], X.at[y, hrows(h)], x_recv.at[y, h]).start()
+
     pl.semaphore_wait(barrier, len(peers))
 
     t_copies = [
@@ -174,15 +175,25 @@
     def xe_copy(m):
         return remote(bufs[m].at[r], bufs[m].at[r], xe_send.at[m], w_recv.at[m, r], xpart)
 
-    def ring_open(m):
-        ring_start(m, 0)
+    def xe_start(m):
         if NX > 1:
-            xe_copy(m).start()
+
+            @pl.when(k == m)
+            def _():
+                xe_copy(m).start()
+
+    def xe_share(m):
+        j = slot_at(1, 0)
+        return remote(bufs[m].at[j], bufs[m].at[j], xe_send.at[2 + m], w_recv.at[m, j], partner)
 
     def ring_second(m):
         if NX > 1:
-            recv_wait(m, (1 - xh) * NZ + z)
+            recv_wait(m, slot_at(1, 0))
             ring_start(m, 1)
+
+            @pl.when(k == m)
+            def _():
+                xe_share(m).start()
 
     def ring_step(m, side, t):
         if NZ == 1 or t > half or side >= NX:
@@ -217,7 +228,12 @@
 
     def ring_drain(m):
         if NX > 1:
-            xe_copy(m).wait_send()
+
+            @pl.when(k == m)
+            def _():
+                xe_copy(m).wait_send()
+                xe_share(m).wait_send()
+
         for side in range(NX):
             for t in range(half):
                 if t < half - 1:
@@ -246,9 +262,9 @@
     below, above, across = (y + 3) % NY, (y + 1) % NY, (y + 2) % NY
     x_sends = [
         x_copy(y, 0, 0, yp),
-        x_copy(y, 1, 1, ym),
-        x_copy(y, 1, 2, yp),
-        x_copy(y, 0, 3, ym),
+        x_copy(y, 0, 1, ym),
+        x_copy(y, 1, 2, ym),
+        x_copy(y, 1, 3, yp),
         x_copy(below, 0, 4, yp),
         x_copy(above, 1, 5, ym),
     ]
@@ -257,7 +273,7 @@
         def chunk(i, carry):
             at = pl.ds(pl.multiple_of(i * CH, CH), CH)
             x = X[slot, at, :].astype(jnp.float32)
-            xn[at, :] = norm_rows(x, mod[1:2, :], mod[0:1, :]).astype(jnp.bfloat16)
+            xn[at, :] = norm_rows(x, mod[1], mod[0]).astype(jnp.bfloat16)
             return carry
 
         lax.fori_loop(0, rows // CH, chunk, 0)
@@ -292,32 +308,59 @@
         buf = (kbuf, vbuf)[which]
         pltpu.make_async_copy(buf.at[:, at], buf.at[:, at], kv_recv.at[which, at]).wait()
 
+    early = k == p
+
+    def when_early(*steps):
+        @pl.when(early)
+        def _():
+            for step in steps:
+                step()
+
+    def when_late(*steps):
+        @pl.when(jnp.logical_not(early))
+        def _():
+            for step in steps:
+                step()
+
+    def own_half(h):
+        x_wait(y, h)
+        x_sends[2 * h].start()
+        x_sends[2 * h + 1].start()
+
+    def pass_below():
+        x_wait(below, 0)
+        x_sends[4].start()
+
+    def pass_above():
+        x_wait(above, 1)
+        x_sends[5].start()
+
+    for c in loc_w:
+        c.wait()
+    ring_start(0, 0)
+    xe_start(0)
+    when_early(lambda: own_half(0), lambda: own_half(1), lambda: layer_in(y))
     position = lax.broadcasted_iota(jnp.int32, (8, 2 * NY * rows), 1)
     bias[...] = jnp.where(position < length[0], 0.0, -1e30)
-    for c in loc_w:
-        c.wait()
-    ring_open(0)
-    x_wait(y, 0)
-    x_sends[0].start()
     ring_step(0, 0, 1)
     ring_second(0)
+    when_late(lambda: own_half(0))
     ring_step(0, 0, 2)
-    x_wait(y, 1)
-    for c in x_sends[1:4]:
-        c.start()
+    when_early(pass_below)
     ring_step(0, 1, 1)
+    when_early(pass_above)
+    when_late(lambda: own_half(1))
+    loc_wo.wait()
+    xe_start(1)
     ring_step(0, 0, 3)
-    layer_in(y)
+    when_late(lambda: layer_in(y))
     ring_step(0, 1, 2)
+    when_late(pass_below, pass_above)
     ring_step(0, 0, 4)
-    x_wait(below, 0)
-    x_sends[4].start()
-    x_wait(above, 1)
-    x_sends[5].start()
     ring_step(0, 1, 3)
+    ring_start(1, 0)
     ring_step(0, 1, 4)
-    loc_wo.wait()
-    ring_open(1)
+    ring_second(1)
     ring_shared(0)
 
     order = (y, below, above, across)
@@ -336,16 +379,18 @@
             c.start()
         kv_copy(1, slot).start()
         if i == 0:
-            ring_second(1)
+            ring_step(1, 0, 1)
         elif i == 1:
-            ring_step(1, 0, 1)
+            ring_step(1, 1, 1)
         elif i == 2:
-            ring_step(1, 1, 1)
+            ring_step(1, 0, 2)
+        else:
+            ring_step(1, 1, 2)
 
     factor = math.log2(math.e) / math.sqrt(DH)
     cols = pl.ds(pl.multiple_of(y * G, G), G)
-    qgain = qg[:, cols] * factor
-    kgain = kg[:, cols]
+    qgain = qg[cols].reshape(1, G) * factor
+    kgain = kg[cols].reshape(1, G)
 
     def finish(slot, which):
         total = ssb[0, slot] + ssb[1, slot] + ssb[2, slot] + ssb[3, slot]
@@ -362,8 +407,8 @@
             pltpu.make_async_copy(ssb.at[src, slot], ssb.at[src, slot], ss_recv.at[src, slot]).wait()
         finish(slot, 0)
         kv_copy(0, slot).start()
-    ring_step(1, 0, 2)
-    ring_step(1, 1, 2)
+    ring_step(1, 0, 3)
+    ring_step(1, 1, 3)
     for which in (1, 0):
         for slot in range(NY):
             kv_wait(which, (1 - k) * NY + slot)
@@ -393,14 +438,12 @@
             attend(slot, h)
             return carry
 
-        lax.fori_loop(0, heads, head, 0)
+        lax.fori_loop(0, heads, head, 0, unroll=True)
         if dev is not None:
             at_copy(n, slot, dev).start()
         if n == 0:
-            ring_step(1, 0, 3)
-            ring_step(1, 1, 3)
+            ring_step(1, 0, 4)
         elif n == 1:
-            ring_step(1, 0, 4)
             ring_step(1, 1, 4)
 
     ring_shared(1)
@@ -422,15 +465,15 @@
     def tail(i, carry):
         at = pl.ds(pl.multiple_of(i * CH, CH), CH)
         x = X[y, at, :].astype(jnp.float32)
-        b = (x + mod[2:3, :] * acc[at, :]).astype(jnp.bfloat16).astype(jnp.float32)
-        xn[at, :] = norm_rows(b, mod[4:5, :], mod[3:4, :]).astype(jnp.bfloat16)
+        b = (x + mod[2] * acc[at, :]).astype(jnp.bfloat16).astype(jnp.float32)
+        xn[at, :] = norm_rows(b, mod[4], mod[3]).astype(jnp.bfloat16)
         return carry
 
     lax.fori_loop(0, rows // CH, tail, 0)
-    vel = jnp.dot(xn[...], whead[...], preferred_element_type=jnp.float32).astype(jnp.bfloat16)
-    C = vel.shape[1] // 2
-    vsend[0, :, :C] = vel[:, :C]
-    vsend[1, :, :C] = vel[:, C:]
+    vel = lax.dot_general(whead[...], xn[...], (((1,), (1,)), ((), ())), preferred_element_type=jnp.float32)
+    C = vel.shape[0] // 2
+    for c in range(2):
+        vsend[c, :, :rows] = vel[c * C : (c + 1) * C].astype(jnp.bfloat16)
 
     for c in range(2):
         here = jnp.logical_and(p == k, k == c)
@@ -445,9 +488,10 @@
 
     for q in range(2):
         pltpu.make_async_copy(vrecv.at[q], vrecv.at[q], v_recv.at[q]).wait()
-    cond = vrecv[0, :, :C].astype(jnp.float32)
-    uncond = vrecv[1, :, :C].astype(jnp.float32)
-    out[...] = uncond + guid[0] * (cond - uncond)
+    cond = vrecv[0, :, :rows].astype(jnp.float32)
+    uncond = vrecv[1, :, :rows].astype(jnp.float32)
+    token = s * rows + lax.broadcasted_iota(jnp.int32, out.shape, 1)
+    out[...] = jnp.where(token < length[0], step[0] * (uncond + guid[0] * (cond - uncond)), 0.0)
 
     @pl.when(k != p)
     def _():
@@ -492,10 +536,10 @@
         vmem = pl.BlockSpec(memory_space=pltpu.VMEM)
         smem = pl.BlockSpec(memory_space=pltpu.SMEM)
         hbm = pl.BlockSpec(memory_space=pl.ANY)
-        guided = pl.pallas_call(
+        change = pl.pallas_call(
             functools.partial(kernel, NX, NZ),
-            out_shape=jax.ShapeDtypeStruct((rows, chans), f32),
-            in_specs=[hbm, hbm, hbm, vmem, vmem, vmem, vmem, smem, smem],
+            out_shape=jax.ShapeDtypeStruct((chans, rows), f32),
+            in_specs=[hbm, hbm, hbm, vmem, vmem, vmem, vmem, smem, smem, smem],
             out_specs=vmem,
             scratch_shapes=[
                 pltpu.VMEM((NY, rows, width), bf),
@@ -510,8 +554,8 @@
                 pltpu.VMEM((NY, heads, rows, DH), bf),
                 pltpu.VMEM((NY, heads, rows, DH), bf),
                 pltpu.VMEM((rows, width), f32),
-                pltpu.VMEM((2, rows, DH), bf),
-                pltpu.VMEM((2, rows, DH), bf),
+                pltpu.VMEM((2, chans, G), bf),
+                pltpu.VMEM((2, chans, G), bf),
                 pltpu.VMEM((8, seq * rows), f32),
                 DMA((NY, 2)),
                 DMA((2,)),
@@ -519,7 +563,7 @@
                 DMA((2, R)),
                 DMA((2, 2, half)),
                 DMA((2, 2, half)),
-                DMA((2,)),
+                DMA((4,)),
                 DMA((4,)),
                 DMA((3, NY)),
                 DMA((NY, NY)),
@@ -538,17 +582,15 @@
             hidden[0, 0],
             w_qkv,
             w_out,
-            modulation[0],
-            q_gain[None],
-            k_gain[None],
-            w_head,
+            jnp.transpose(modulation, (1, 0, 2)),
+            q_gain,
+            k_gain,
+            w_head.T,
             lengths,
             guidance,
+            step_size,
         )
-        position = lax.axis_index("seq")
-        valid = position * rows + jnp.arange(rows, dtype=jnp.int32) < lengths[0]
-        current = latent[0]
-        return jnp.where(valid[:, None], current - step_size[0] * guided, current)[None]
+        return (latent[0].T - change).T[None]
 
     return jax.shard_map(
         local,

time: 111 us -> 96 us (0.86)
  Pallas kernels: 104 us -> 91.8 us
  local copies, waits for them, and re-layouts: 4.72 us -> 0.01 us
  other arithmetic: 0.11 us -> 1.43 us
    pallas_call x1, Pallas kernels: 104 us -> 91.8 us  [local(): pl.pallas_call(functools.partial(kernel, NX, NZ), out_shape=jax.ShapeDtyp...]
    unnamed x13 -> x2, local copies, waits for them, and re-layouts: 2.8 us -> 0.01 us
    broadcast_in_dim x3 -> x0, local copies, waits for them, and re-layouts: 1.92 us -> none  [the longest x1 0.73 us: local(): jnp.where(valid[:, None], current - step_size[0] * guided, current)[None]]
    broadcast_in_dim x1, other arithmetic: 0.1 us -> 1.43 us  [local(): return (latent[0].T - change).T[None]]
where the time goes in v2:
time: 96 us; the launch traced here: 95.2 us
  Pallas kernels  91.8 us (96%)
  between operations  1.97 us (2%)
  other arithmetic  1.43 us (1%)
    pallas_call x1, Pallas kernels, local(): pl.pallas_call(functools.partial(kernel, NX, NZ), out_shape=jax.ShapeDtyp...  91.8 us

profile of v2, /device:TPU:1, one launch (start us, length us, event | category | flops | bytes accessed | tf_op | source)
XLA Modules:
  0.0 95.2 jit_solution(11472575143237819327)
XLA Ops:
  1.9 0.0 copy-start
  2.0 91.8 %block.1 = f32[32,288]{1,0:T(8,128)} custom-call(bf16[288,1536]{1,0:T(8,128)(2,1)} %bitcast.13, bf16[96,4608]{1,0:T(8,128)(2,1)} %wqkv.1, bf16[96,1536]{1,0:T(8,128)(2,1)} %wout.1, f32[5,1,1536]{2,1,0:T(1,128)} %bitcast.15, f32[1536]{0:T(1024)} %qg.1, f32[1536]{0:T(1024)} %kg.1, bf16[64,1536]{1,0:T(8,128)(2,1)} %bitcast.14, s32[1]{0:T(128)S(6)} %copy.12.length, ...), custom_call_target="tpu_custom_call" | custom-call | tf_op jit(solution)/shard_map/block/pallas_call | solution.py:539
  93.8 0.0 copy-done
  93.8 1.4 %fusion = f32[1,288,32]{1,2,0:T(8,128)} fusion(f32[32,288]{1,0:T(8,128)} %block.1, f32[1,288,32]{1,2,0:T(8,128)S(1)} %copy-done), kind=kLoop, calls=%fused_computation.1 | loop fusion | flops 9216 | bytes 110592 | tf_op jit(solution)/shard_map/broadcast_in_dim | solution.py:593
Async XLA Ops:
  1.9 91.9 %copy-start = (f32[1,288,32]{1,2,0:T(8,128)S(1)}, f32[1,288,32]{1,2,0:T(8,128)}, u32[]{:S(2)}) copy-start(f32[1,288,32]{1,2,0:T(8,128)} %param.12) | copy-start | bytes 110596

commit v3 on v2

--- a/solution.py
+++ b/solution.py
@@ -87,7 +87,7 @@
     transposed = (p, r, k * NY + y)
     partner = (1 - k, r, s)
     xpart = (k, (1 - xh) * NZ + z, s)
-    znext = (k, xh * NZ + (z + 1 + k * (NZ - 2)) % NZ, s)
+    znext = ((k, xh * NZ + (z + 1) % NZ, s), (k, xh * NZ + (z + NZ - 1) % NZ, s))
 
     def remote(src, dst, ssem, rsem, dev):
         return pltpu.make_async_remote_copy(
@@ -144,114 +144,88 @@
 
     bufs = (W, WO)
 
-    def slot_at(side, t):
+    def slot_at(way, side, t):
         other = xh if side == 0 else 1 - xh
-        return other * NZ + (z + t * (NZ - 1) + k * 2 * t) % NZ
-
-    def ring_copy(m, side, t):
-        j = slot_at(side, t)
-        return remote(bufs[m].at[j], bufs[m].at[j], ring_send.at[m, side, t], w_recv.at[m, j], znext)
-
-    def share_copy(m, side, t):
-        j = slot_at(side, t)
-        return remote(bufs[m].at[j], bufs[m].at[j], share_send.at[m, side, t - 1], w_recv.at[m, j], partner)
-
-    def mine(side):
-        return (xh if side == 0 else 1 - xh) == k
+        return other * NZ + (z + (t if way else t * (NZ - 1))) % NZ
+
+    def ring_copy(m, way, side, t):
+        j = slot_at(way, side, t)
+        return remote(bufs[m].at[j], bufs[m].at[j], ring_send.at[m, way, side, t], w_recv.at[m, j], znext[way])
+
+    def share_copy(m, way, side, t):
+        j = slot_at(way, side, t)
+        return remote(bufs[m].at[j], bufs[m].at[j], share_send.at[m, way, side, t - 1], w_recv.at[m, j], partner)
+
+    def farthest(way, side):
+        return (xh if side == 0 else 1 - xh) == way
 
     def recv_wait(m, j):
         pltpu.make_async_copy(bufs[m].at[j], bufs[m].at[j], w_recv.at[m, j]).wait()
 
     def ring_start(m, side):
-        if NZ > 1:
-            if half > 1:
-                ring_copy(m, side, 0).start()
-            else:
-
-                @pl.when(mine(side))
-                def _():
-                    ring_copy(m, side, 0).start()
+        for way in range(2 if NZ > 1 else 0):
+            ring_copy(m, way, side, 0).start()
 
     def xe_copy(m):
         return remote(bufs[m].at[r], bufs[m].at[r], xe_send.at[m], w_recv.at[m, r], xpart)
 
+    def xe_share(m):
+        j = slot_at(0, 1, 0)
+        return remote(bufs[m].at[j], bufs[m].at[j], xe_send.at[2 + m], w_recv.at[m, j], partner)
+
     def xe_start(m):
         if NX > 1:
-
-            @pl.when(k == m)
-            def _():
-                xe_copy(m).start()
-
-    def xe_share(m):
-        j = slot_at(1, 0)
-        return remote(bufs[m].at[j], bufs[m].at[j], xe_send.at[2 + m], w_recv.at[m, j], partner)
+            xe_copy(m).start()
 
     def ring_second(m):
         if NX > 1:
-            recv_wait(m, slot_at(1, 0))
+            recv_wait(m, slot_at(0, 1, 0))
             ring_start(m, 1)
-
-            @pl.when(k == m)
-            def _():
-                xe_share(m).start()
+            xe_share(m).start()
 
     def ring_step(m, side, t):
-        if NZ == 1 or t > half or side >= NX:
+        if NZ == 1:
             return
-
-        def go():
-            recv_wait(m, slot_at(side, t))
-            if t < half - 1:
-                ring_copy(m, side, t).start()
-            elif t == half - 1:
-
-                @pl.when(mine(side))
-                def _():
-                    ring_copy(m, side, t).start()
-
-            share_copy(m, side, t).start()
-
-        if t < half:
-            go()
-        else:
-            pl.when(mine(side))(go)
+        for way in range(2):
+
+            def go(way=way):
+                recv_wait(m, slot_at(way, side, t))
+                if t < half - 1:
+                    ring_copy(m, way, side, t).start()
+                elif t == half - 1:
+
+                    @pl.when(farthest(way, side))
+                    def _():
+                        ring_copy(m, way, side, t).start()
+
+                share_copy(m, way, side, t).start()
+
+            if t < half:
+                go()
+            else:
+                pl.when(farthest(way, side))(go)
 
     def ring_shared(m):
         for side in range(NX):
-            for t in range(half + 1, NZ):
-                recv_wait(m, slot_at(side, t))
-            if NZ > 1:
-
-                @pl.when(jnp.logical_not(mine(side)))
-                def _():
-                    recv_wait(m, slot_at(side, half))
+            for t in range(NZ):
+                if side or t:
+                    recv_wait(m, slot_at(1, side, t))
 
     def ring_drain(m):
         if NX > 1:
-
-            @pl.when(k == m)
-            def _():
-                xe_copy(m).wait_send()
-                xe_share(m).wait_send()
-
-        for side in range(NX):
-            for t in range(half):
-                if t < half - 1:
-                    ring_copy(m, side, t).wait_send()
-                else:
-
-                    @pl.when(mine(side))
-                    def _():
-                        ring_copy(m, side, t).wait_send()
-
-            for t in range(1, half + 1):
-                if t < half:
-                    share_copy(m, side, t).wait_send()
-                else:
-
-                    @pl.when(mine(side))
-                    def _():
-                        share_copy(m, side, t).wait_send()
+            xe_copy(m).wait_send()
+            xe_share(m).wait_send()
+        for way in range(2 if NZ > 1 else 0):
+            for side in range(NX):
+                for t in range(half - 1):
+                    ring_copy(m, way, side, t).wait_send()
+                for t in range(1, half):
+                    share_copy(m, way, side, t).wait_send()
+
+                @pl.when(farthest(way, side))
+                def _():
+                    ring_copy(m, way, side, half - 1).wait_send()
+                    share_copy(m, way, side, half).wait_send()
 
     def x_copy(slot, h, n, dev):
         return remote(X.at[slot, hrows(h)], X.at[slot, hrows(h)], y_send.at[n], x_recv.at[slot, h], dev)
@@ -337,31 +311,41 @@
 
     for c in loc_w:
         c.wait()
-    ring_start(0, 0)
-    xe_start(0)
-    when_early(lambda: own_half(0), lambda: own_half(1), lambda: layer_in(y))
+    when_early(
+        lambda: ring_start(0, 0),
+        lambda: xe_start(0),
+        lambda: own_half(0),
+        lambda: own_half(1),
+        lambda: layer_in(y),
+    )
     position = lax.broadcasted_iota(jnp.int32, (8, 2 * NY * rows), 1)
     bias[...] = jnp.where(position < length[0], 0.0, -1e30)
-    ring_step(0, 0, 1)
-    ring_second(0)
-    when_late(lambda: own_half(0))
-    ring_step(0, 0, 2)
-    when_early(pass_below)
-    ring_step(0, 1, 1)
-    when_early(pass_above)
-    when_late(lambda: own_half(1))
     loc_wo.wait()
-    xe_start(1)
-    ring_step(0, 0, 3)
-    when_late(lambda: layer_in(y))
-    ring_step(0, 1, 2)
-    when_late(pass_below, pass_above)
-    ring_step(0, 0, 4)
-    ring_step(0, 1, 3)
-    ring_start(1, 0)
-    ring_step(0, 1, 4)
-    ring_second(1)
-    ring_shared(0)
+    when_early(
+        lambda: ring_step(0, 0, 1),
+        lambda: ring_second(0),
+        lambda: ring_step(0, 0, 2),
+        pass_below,
+        lambda: ring_step(0, 1, 1),
+        pass_above,
+        lambda: ring_step(0, 0, 3),
+        lambda: ring_step(0, 1, 2),
+        lambda: ring_step(0, 0, 4),
+        lambda: ring_step(0, 1, 3),
+        lambda: ring_step(0, 1, 4),
+    )
+    when_late(
+        lambda: own_half(0),
+        lambda: own_half(1),
+        lambda: xe_start(1),
+        lambda: layer_in(y),
+        lambda: ring_start(1, 0),
+        pass_below,
+        pass_above,
+        lambda: ring_second(1),
+        lambda: ring_step(1, 0, 1),
+        lambda: ring_shared(0),
+    )
 
     order = (y, below, above, across)
     for i, slot in enumerate(order):
@@ -378,14 +362,8 @@
         for c in ss_copies(slot):
             c.start()
         kv_copy(1, slot).start()
-        if i == 0:
-            ring_step(1, 0, 1)
-        elif i == 1:
-            ring_step(1, 1, 1)
-        elif i == 2:
-            ring_step(1, 0, 2)
-        else:
-            ring_step(1, 1, 2)
+        side, t = ((1, 1), (0, 2), (1, 2), (0, 3))[i]
+        when_late(lambda: ring_step(1, side, t))
 
     factor = math.log2(math.e) / math.sqrt(DH)
     cols = pl.ds(pl.multiple_of(y * G, G), G)
@@ -407,8 +385,7 @@
             pltpu.make_async_copy(ssb.at[src, slot], ssb.at[src, slot], ss_recv.at[src, slot]).wait()
         finish(slot, 0)
         kv_copy(0, slot).start()
-    ring_step(1, 0, 3)
-    ring_step(1, 1, 3)
+    when_late(lambda: ring_step(1, 1, 3))
     for which in (1, 0):
         for slot in range(NY):
             kv_wait(which, (1 - k) * NY + slot)
@@ -441,12 +418,10 @@
         lax.fori_loop(0, heads, head, 0, unroll=True)
         if dev is not None:
             at_copy(n, slot, dev).start()
-        if n == 0:
-            ring_step(1, 0, 4)
-        elif n == 1:
-            ring_step(1, 1, 4)
-
-    ring_shared(1)
+        if n < 2:
+            when_late(lambda: ring_step(1, n, 4))
+
+    when_early(lambda: ring_shared(1))
     per = R // NY if R >= NY else 1
 
     def out_rows(g):
@@ -500,8 +475,8 @@
 
     for c in x_sends:
         c.wait_send()
-    for m in range(2):
-        ring_drain(m)
+    when_early(lambda: ring_drain(0))
+    when_late(lambda: ring_drain(1))
     for slot in range(NY):
         for c in ss_copies(slot):
             c.wait_send()
@@ -561,8 +536,8 @@
                 DMA((2,)),
                 DMA((6,)),
                 DMA((2, R)),
-                DMA((2, 2, half)),
-                DMA((2, 2, half)),
+                DMA((2, 2, 2, half)),
+                DMA((2, 2, 2, half)),
                 DMA((4,)),
                 DMA((4,)),
                 DMA((3, NY)),

time: 96 us -> 90.9 us (0.947)
  Pallas kernels: 91.8 us -> 87.3 us
    pallas_call x1, Pallas kernels: 91.8 us -> 87.3 us  [local(): pl.pallas_call(functools.partial(kernel, NX, NZ), out_shape=jax.ShapeDtyp...]
where the time goes in v3:
time: 90.9 us; the launch traced here: 90.7 us
  Pallas kernels  87.3 us (96%)
  between operations  1.97 us (2%)
  other arithmetic  1.43 us (2%)
    pallas_call x1, Pallas kernels, local(): pl.pallas_call(functools.partial(kernel, NX, NZ), out_shape=jax.ShapeDtyp...  87.3 us

profile of v3, /device:TPU:1, one launch (start us, length us, event | category | flops | bytes accessed | tf_op | source)
XLA Modules:
  0.0 90.7 jit_solution(17623398354773117432)
XLA Ops:
  1.9 0.0 copy-start
  2.0 87.3 %block.1 = f32[32,288]{1,0:T(8,128)} custom-call(bf16[288,1536]{1,0:T(8,128)(2,1)} %bitcast.13, bf16[96,4608]{1,0:T(8,128)(2,1)} %wqkv.1, bf16[96,1536]{1,0:T(8,128)(2,1)} %wout.1, f32[5,1,1536]{2,1,0:T(1,128)} %bitcast.15, f32[1536]{0:T(1024)} %qg.1, f32[1536]{0:T(1024)} %kg.1, bf16[64,1536]{1,0:T(8,128)(2,1)} %bitcast.14, s32[1]{0:T(128)S(6)} %copy.12.length, ...), custom_call_target="tpu_custom_call" | custom-call | tf_op jit(solution)/shard_map/block/pallas_call | solution.py:514
  89.3 0.0 copy-done
  89.3 1.4 %fusion = f32[1,288,32]{1,2,0:T(8,128)} fusion(f32[32,288]{1,0:T(8,128)} %block.1, f32[1,288,32]{1,2,0:T(8,128)S(1)} %copy-done), kind=kLoop, calls=%fused_computation.1 | loop fusion | flops 9216 | bytes 110592 | tf_op jit(solution)/shard_map/broadcast_in_dim | solution.py:568
Async XLA Ops:
  1.9 87.3 %copy-start = (f32[1,288,32]{1,2,0:T(8,128)S(1)}, f32[1,288,32]{1,2,0:T(8,128)}, u32[]{:S(2)}) copy-start(f32[1,288,32]{1,2,0:T(8,128)} %param.12) | copy-start | bytes 110596
